TPU v7x, 256 devices: a whole 4x4x8 slice. The times are simulated.
256 devices in a mesh: feat: 32 (over y, z), dp: 8 (over x, core).
Axes of the slice: x: 4, y: 4, z: 8, core: 2. Of those that a mesh axis runs over, the one named last changes fastest.
Arguments:
- face_grid: bfloat16 [32768, 10240], P('dp', 'feat'), may hold values from -6 to 6
- first_nbrs: int32 [16384, 8], P('dp'), may hold values from 0 to 4095
- first_count: int32 [16384], P('dp'), may hold values from 1 to 8
- w_first: bfloat16 [10240, 256], P('feat'), may hold values from -0.0625 to 0.0625
- b_first: float32 [256], replicated, may hold values from -3 to 3
- send_rows: int32 [4096], P('dp'), may hold values from 0 to 2047
- second_nbrs: int32 [16384, 8], P(('dp', 'feat')), may hold values from 0 to 2559
- second_count: int32 [16384], P(('dp', 'feat')), may hold values from 1 to 8
- w_in: bfloat16 [256, 1024], replicated, may hold values from -0.375 to 0.375
- w_out: bfloat16 [1024, 256], replicated, may hold values from -0.1875 to 0.1875
- out_grad: bfloat16 [16384, 256], P(('dp', 'feat')), may hold values from -6 to 6
Outputs:
- embed: bfloat16 [16384, 256], P(('dp', 'feat'))
- grad_first: float32 [10240, 256], P('feat')
Inputs may be any that keep to these rules, and one draw needn't show every extreme that they name: `first_count`: slots at or past a target's count are ignored; counts lie in 1 to 8. `first_nbrs`: only slots below first_count are read. `second_count`: slots at or past a target's count are ignored. `second_nbrs`: indices below 2048 name the partition's own targets, the rest the faces received from the previous partition in order; only slots below second_count are read. `send_rows`: entries may repeat.
All inputs are finite; a program needn't handle non-finite values.
Results may differ from a plain program's by a relative error of at most 0.0061.
Values may be sent and summed in bfloat16 or wider, within the bound.
No kernel may reach another device: no remote copies, remote signals or barrier semaphores. Data moves between devices by JAX's collectives and lax.ppermute only.
A program may use at most 64 MiB of HBM per device.

v0:
```python
import jax
import jax.numpy as jnp
from jax import lax
from jax.sharding import PartitionSpec as P


def passed_along(shard, axis, by):
    devices = lax.axis_size(axis)
    return lax.ppermute(shard, axis, [(i, (i + by) % devices) for i in range(devices)])


def slope(value):
    sig = jax.nn.sigmoid(value)
    return sig * (1.0 + value * (1.0 - sig))


def mean_rows(table, nbrs, count):
    total = jnp.zeros((nbrs.shape[0], table.shape[1]), jnp.float32)
    for slot in range(nbrs.shape[1]):
        picked = table[nbrs[:, slot]].astype(jnp.float32)
        total = total + jnp.where((slot < count)[:, None], picked, 0.0)
    return total / count[:, None].astype(jnp.float32)


def spread(grad, nbrs, count, size):
    slots = jnp.arange(nbrs.shape[1], dtype=jnp.int32)
    factor = jnp.where(
        slots[None, :] < count[:, None], 1.0 / count[:, None].astype(jnp.float32), 0.0
    )
    terms = (grad[:, None, :] * factor[:, :, None]).reshape(-1, grad.shape[1])
    return jax.ops.segment_sum(terms, nbrs.reshape(-1), num_segments=size)


def body(
    face_grid,
    first_nbrs,
    first_count,
    w_first,
    b_first,
    send_rows,
    second_nbrs,
    second_count,
    w_in,
    w_out,
    out_grad,
):
    targets = first_nbrs.shape[0]
    agg_first = (
        face_grid[:targets].astype(jnp.float32) + mean_rows(face_grid, first_nbrs, first_count)
    ).astype(jnp.bfloat16)
    partial_value = jnp.dot(agg_first, w_first, preferred_element_type=jnp.float32)
    pre_own = lax.psum_scatter(partial_value, "feat", scatter_dimension=0, tiled=True) + b_first
    hidden_own = jax.nn.silu(pre_own).astype(jnp.bfloat16)
    table = lax.all_gather(hidden_own, "feat", axis=0, tiled=True)
    received = passed_along(table[send_rows], "dp", 1)
    extended = jnp.concatenate([table, received], axis=0)
    agg_second = (
        hidden_own.astype(jnp.float32) + mean_rows(extended, second_nbrs, second_count)
    ).astype(jnp.bfloat16)
    pre_mlp = jnp.dot(agg_second, w_in, preferred_element_type=jnp.float32)
    act_mlp = jax.nn.silu(pre_mlp).astype(jnp.bfloat16)
    embed = (
        hidden_own.astype(jnp.float32) + jnp.dot(act_mlp, w_out, preferred_element_type=jnp.float32)
    ).astype(jnp.bfloat16)
    grad_act = lax.dot_general(
        out_grad, w_out, (((1,), (1,)), ((), ())), preferred_element_type=jnp.float32
    )
    grad_pre_mlp = (grad_act * slope(pre_mlp)).astype(jnp.bfloat16)
    grad_agg = lax.dot_general(
        grad_pre_mlp, w_in, (((1,), (1,)), ((), ())), preferred_element_type=jnp.float32
    )
    grad_ext = spread(grad_agg, second_nbrs, second_count, extended.shape[0])
    full_rows = table.shape[0]
    returned = passed_along(grad_ext[full_rows:].astype(jnp.bfloat16), "dp", -1).astype(jnp.float32)
    table_grad = grad_ext[:full_rows].at[send_rows].add(returned)
    own_terms = out_grad.astype(jnp.float32) + grad_agg
    grad_own = (
        lax.psum_scatter(
            table_grad.astype(jnp.bfloat16), "feat", scatter_dimension=0, tiled=True
        ).astype(jnp.float32)
        + own_terms
    )
    grad_pre_own = (grad_own * slope(pre_own)).astype(jnp.bfloat16)
    grad_pre_first = lax.all_gather(grad_pre_own, "feat", axis=0, tiled=True)
    slice_grad = lax.dot_general(
        agg_first, grad_pre_first, (((0,), (0,)), ((), ())), preferred_element_type=jnp.float32
    )
    grad_first = lax.psum(slice_grad, "dp")
    return (embed, grad_first)


def solution(mesh):
    return jax.shard_map(
        body,
        mesh=mesh,
        in_specs=(
            P("dp", "feat"),
            P("dp", None),
            P("dp"),
            P("feat", None),
            P(),
            P("dp"),
            P(("dp", "feat"), None),
            P(("dp", "feat")),
            P(),
            P(),
            P(("dp", "feat"), None),
        ),
        out_specs=(P(("dp", "feat"), None), P("feat", None)),
        check_vma=False,
    )
```

profile of v0, /device:TPU:8, one launch (start us, length us, event | category | flops | bytes accessed | tf_op | source)
XLA Modules:
  0.0 828.4 jit_solution(5859287706951482798)
XLA Ops:
  8.7 4.6 copy.22
  13.4 11.2 %gather_fusion = bf16[2048,320]{1,0:T(8,128)(2,1)} fusion(bf16[4096,320]{1,0:T(8,128)(2,1)} %copy.22, s32[2048]{0:T(1024)S(1)} %broadcast_clamp_fusion.7), kind=kCustom, calls=%fused_computation | custom fusion | bytes 2629632 | tf_op jit(solution)/shard_map/gather | solution.py:20
  24.6 11.2 %gather_fusion.1 = bf16[2048,320]{1,0:T(8,128)(2,1)} fusion(bf16[4096,320]{1,0:T(8,128)(2,1)} %copy.22, s32[2048]{0:T(1024)S(1)} %broadcast_clamp_fusion.6), kind=kCustom, calls=%fused_computation.1 | custom fusion | bytes 2629632 | tf_op jit(solution)/shard_map/gather | solution.py:20
  35.8 11.2 %gather_fusion.2 = bf16[2048,320]{1,0:T(8,128)(2,1)} fusion(bf16[4096,320]{1,0:T(8,128)(2,1)} %copy.22, s32[2048]{0:T(1024)S(1)} %broadcast_clamp_fusion.5), kind=kCustom, calls=%fused_computation.2 | custom fusion | bytes 2629632 | tf_op jit(solution)/shard_map/gather | solution.py:20
  47.0 11.2 %gather_fusion.3 = bf16[2048,320]{1,0:T(8,128)(2,1)} fusion(bf16[4096,320]{1,0:T(8,128)(2,1)} %copy.22, s32[2048]{0:T(1024)S(1)} %broadcast_clamp_fusion.4), kind=kCustom, calls=%fused_computation.3 | custom fusion | bytes 2629632 | tf_op jit(solution)/shard_map/gather | solution.py:20
  58.1 11.2 %gather_fusion.4 = bf16[2048,320]{1,0:T(8,128)(2,1)} fusion(bf16[4096,320]{1,0:T(8,128)(2,1)} %copy.22, s32[2048]{0:T(1024)S(1)} %broadcast_clamp_fusion.3), kind=kCustom, calls=%fused_computation.4 | custom fusion | bytes 2629632 | tf_op jit(solution)/shard_map/gather | solution.py:20
  69.3 11.2 %gather_fusion.5 = bf16[2048,320]{1,0:T(8,128)(2,1)} fusion(bf16[4096,320]{1,0:T(8,128)(2,1)} %copy.22, s32[2048]{0:T(1024)S(1)} %broadcast_clamp_fusion.2), kind=kCustom, calls=%fused_computation.5 | custom fusion | bytes 2629632 | tf_op jit(solution)/shard_map/gather | solution.py:20
  80.5 11.2 %gather_fusion.6 = bf16[2048,320]{1,0:T(8,128)(2,1)} fusion(bf16[4096,320]{1,0:T(8,128)(2,1)} %copy.22, s32[2048]{0:T(1024)S(1)} %broadcast_clamp_fusion.1), kind=kCustom, calls=%fused_computation.6 | custom fusion | bytes 2629632 | tf_op jit(solution)/shard_map/gather | solution.py:20
  91.7 11.2 %gather_fusion.7 = bf16[2048,320]{1,0:T(8,128)(2,1)} fusion(bf16[4096,320]{1,0:T(8,128)(2,1)} %copy.22, s32[2048]{0:T(1024)S(1)} %broadcast_clamp_fusion), kind=kCustom, calls=%fused_computation.7 | custom fusion | bytes 2629632 | tf_op jit(solution)/shard_map/gather | solution.py:20
  102.8 8.9 %add_convert_fusion = bf16[2048,320]{1,0:T(8,128)(2,1)S(1)} fusion(bf16[2048,320]{1,0:T(8,128)(2,1)} %gather_fusion.7, bf16[2048,320]{1,0:T(8,128)(2,1)} %gather_fusion.6, bf16[2048,320]{1,0:T(8,128)(2,1)} %gather_fusion.5, bf16[2048,320]{1,0:T(8,128)(2,1)} %gather_fusion.4, bf16[2048,320]{1,0:T(8,128)(2,1)} %gather_fusion.3, ...), kind=kLoop, calls=%fused_computation.19 | loop fusion | flops 17694720 | bytes 13131776 | tf_op jit(solution)/shard_map/convert_element_type | solution.py:50
  111.8 2.0 fusion.40
  113.9 220.8 %reduce-scatter.3.cloned.1.call-done = f32[64,256]{1,0:T(8,128)} async-done(((f32[2048,256]{1,0:T(8,128)}), f32[64,256]{1,0:T(8,128)}) %reduce-scatter.3.cloned.1.call-update) | async-done | bytes 65552 | tf_op jit(solution)/shard_map/reduce_scatter | solution.py:52
  336.6 75.6 %all-gather.3.cloned.1.call-done = bf16[2048,256]{1,0:T(8,128)(2,1)} async-done(((bf16[64,256]{1,0:T(8,128)(2,1)}), bf16[2048,256]{1,0:T(8,128)(2,1)}) %all-gather.3.cloned.1.call-update) | async-done | bytes 1048592 | tf_op jit(solution)/shard_map/all_gather | solution.py:54
  412.2 3.6 gather_fusion.8
  417.3 5.8 collective-permute-done
  423.8 2.1 gather_fusion.10
  426.0 2.2 gather_fusion.11
  428.2 2.1 gather_fusion.12
  430.3 2.1 gather_fusion.13
  432.5 2.1 gather_fusion.14
  434.6 2.1 gather_fusion.15
  436.8 2.1 gather_fusion.9
  438.9 2.1 gather_fusion.16
  441.9 5.1 scatter_custom_fusion
  448.1 3.1 slice.112
  451.9 6.0 scatter_custom_fusion.1
  457.9 2.7 convert_element_type.125
  460.7 215.0 %reduce-scatter.5.cloned.1.call-done = bf16[64,256]{1,0:T(8,128)(2,1)} async-done(((bf16[2048,256]{1,0:T(8,128)(2,1)}), bf16[64,256]{1,0:T(8,128)(2,1)}) %reduce-scatter.5.cloned.1.call-update) | async-done | bytes 32784 | tf_op jit(solution)/shard_map/reduce_scatter | solution.py:78
  677.2 75.9 %all-gather.5.cloned.1.call-done = bf16[2048,256]{1,0:T(8,128)(2,1)} async-done(((bf16[64,256]{1,0:T(8,128)(2,1)}), bf16[2048,256]{1,0:T(8,128)(2,1)}) %all-gather.5.cloned.1.call-update) | async-done | bytes 1048592 | tf_op jit(solution)/shard_map/all_gather | solution.py:84
  753.1 2.5 fusion.41
  756.6 63.6 %all-reduce.2.cloned.1.call-done = f32[320,256]{1,0:T(8,128)} async-done(((f32[320,256]{1,0:T(8,128)}), f32[320,256]{1,0:T(8,128)}) %all-reduce.2.cloned.1.call-update) | async-done | bytes 327696 | tf_op jit(solution)/shard_map/psum | solution.py:88
  820.1 1.7 copy.35
  (70 shorter events, 10.7 us)
Async XLA Ops:
  7.2 433.9 %copy-start = (bf16[256,1024]{1,0:T(8,128)(2,1)S(1)}, bf16[256,1024]{1,0:T(8,128)(2,1)}, u32[]{:S(2)}) copy-start(bf16[256,1024]{1,0:T(8,128)(2,1)} %param.19) | copy-start | bytes 1572868
  7.2 327.5 %reduce-scatter.3.cloned.1.call-start = ((), (), s32[]{:S(2)}) async-start(), calls=%async_computation.2 | async-start | bytes 2162688 | tf_op jit(solution)/shard_map/reduce_scatter | solution.py:52
  8.7 4.6 copy-start.5
  102.8 8.9 %copy-start.3 = (bf16[320,256]{1,0:T(8,128)(2,1)S(1)}, bf16[320,256]{1,0:T(8,128)(2,1)}, u32[]{:S(2)}) copy-start(bf16[320,256]{1,0:T(8,128)(2,1)} %param.14) | copy-start | bytes 491524
  113.8 220.9 %copy-start.8 = (f32[256]{0:T(256)S(1)}, f32[256]{0:T(256)}, u32[]{:S(2)}) copy-start(f32[256]{0:T(256)} %param.15) | copy-start | bytes 3076
  113.8 222.6 %copy-start.10 = (s32[512]{0:T(512)S(1)}, s32[512]{0:T(512)}, u32[]{:S(2)}) copy-start(s32[512]{0:T(512)} %param.16) | copy-start | bytes 6148
  113.8 222.7 %copy-start.7 = (s32[64,8]{0,1:T(8,128)S(1)}, s32[64,8]{0,1:T(8,128)}, u32[]{:S(2)}) copy-start(s32[64,8]{0,1:T(8,128)} %param.17) | copy-start | bytes 6148
  113.8 222.7 %copy-start.9 = (s32[64]{0:T(128)S(1)}, s32[64]{0:T(128)}, u32[]{:S(2)}) copy-start(s32[64]{0:T(128)} %param.18) | copy-start | bytes 772
  113.8 298.4 %all-gather.3.cloned.1.call-start = ((), (), s32[]{:S(2)}) async-start(), calls=%async_computation.3 | async-start | bytes 1081344 | tf_op jit(solution)/shard_map/all_gather | solution.py:54
  336.2 339.6 %reduce-scatter.5.cloned.1.call-start = ((), (), s32[]{:S(2)}) async-start(), calls=%async_computation.4 | async-start | bytes 1081344 | tf_op jit(solution)/shard_map/reduce_scatter | solution.py:78
  412.2 3.9 copy-start.1
  415.9 7.2 collective-permute-start
  417.3 23.8 %copy-start.4 = (bf16[64,256]{1,0:T(8,128)(2,1)S(1)}, bf16[64,256]{1,0:T(8,128)(2,1)}, u32[]{:S(2)}) copy-start(bf16[64,256]{1,0:T(8,128)(2,1)} %multiply_convert_fusion.3) | copy-start | bytes 98308
  426.0 15.4 %copy-start.6 = (bf16[64,256]{1,0:T(8,128)(2,1)S(1)}, bf16[64,256]{1,0:T(8,128)(2,1)}, u32[]{:S(2)}) copy-start(bf16[64,256]{1,0:T(8,128)(2,1)} %param.21) | copy-start | bytes 98308
  426.0 15.4 %copy-start.11 = (bf16[1024,256]{1,0:T(8,128)(2,1)S(1)}, bf16[1024,256]{1,0:T(8,128)(2,1)}, u32[]{:S(2)}) copy-start(bf16[1024,256]{1,0:T(8,128)(2,1)} %param.20) | copy-start | bytes 1572868
  448.0 3.9 collective-permute-start.1
  457.9 217.8 %copy-start.2 = (f32[64,256]{1,0:T(8,128)S(1)}, f32[64,256]{1,0:T(8,128)}, u32[]{:S(2)}) copy-start(f32[64,256]{1,0:T(8,128)} %reduce-scatter.3.cloned.1.call-done) | copy-start | bytes 196612
  460.7 292.5 %all-gather.5.cloned.1.call-start = ((), (), s32[]{:S(2)}) async-start(), calls=%async_computation.5 | async-start | bytes 1081344 | tf_op jit(solution)/shard_map/all_gather | solution.py:84
  677.2 142.9 %all-reduce.2.cloned.1.call-start = ((), (), s32[]{:S(2)}) async-start(), calls=%async_computation.6 | async-start | bytes 655360 | tf_op jit(solution)/shard_map/psum | solution.py:88
Sparse Core Ops, SparseCore 0:
  113.9 220.6 reduce-scatter.2
  337.8 74.3 all-gather.2
  460.8 214.9 reduce-scatter.4
  678.8 74.3 all-gather.4
  755.9 64.2 all-reduce.1
where the time goes:
time: 830 us; the launch traced here: 828 us
  waiting for transfers between devices  658 us (79%)
  local copies, waits for them, and re-layouts  123 us (15%)
  other arithmetic  27.3 us (3%)
  between operations  14 us (2%)
    reduce_scatter x1, waiting for transfers between devices, body(): lax.psum_scatter(partial_value, 'feat', scatter_dimension=0, tiled=True)  221 us
    reduce_scatter x1, waiting for transfers between devices, body(): lax.psum_scatter(table_grad.astype(jnp.bfloat16), 'feat', scatter_dimensi...  215 us
    gather x16, local copies, waits for them, and re-layouts, mean_rows(): picked = table[nbrs[:, slot]].astype(jnp.float32)  107 us
    all_gather x1, waiting for transfers between devices, body(): grad_pre_first = lax.all_gather(grad_pre_own, 'feat', axis=0, tiled=True)  75.9 us
    all_gather x1, waiting for transfers between devices, body(): table = lax.all_gather(hidden_own, 'feat', axis=0, tiled=True)  75.6 us
    psum x1, waiting for transfers between devices, body(): grad_first = lax.psum(slice_grad, 'dp')  63.6 us
  transfers between devices with their start and end apart: 7, of which 7 were waited for; matrix products, arithmetic and copies ran while one was open for 1% of the time, Pallas kernels for 0%

commit v1 on v0

--- a/solution.py
+++ b/solution.py
@@ -85,7 +85,13 @@
     slice_grad = lax.dot_general(
         agg_first, grad_pre_first, (((0,), (0,)), ((), ())), preferred_element_type=jnp.float32
     )
-    grad_first = lax.psum(slice_grad, "dp")
+    n_dev = lax.axis_size("dp")
+    grad_first, far = (slice_grad, 1)
+    while far < n_dev:
+        grad_first = grad_first + lax.ppermute(
+            grad_first, "dp", [(i_2, i_2 ^ far) for i_2 in range(n_dev)]
+        )
+        far = 2 * far
     return (embed, grad_first)
 
 

time: 830 us -> 787 us (0.948)
  waiting for transfers between devices: 658 us -> 611 us
    psum x1 -> x0, waiting for transfers between devices: 63.6 us -> none  [body(): grad_first = lax.psum(slice_grad, 'dp')]
    ppermute x0 -> x3, waiting for transfers between devices: none -> 16.5 us  [body(): lax.ppermute(grad_first, 'dp', [(i_2, i_2 ^ far) for i_2 in range(n_dev)])]
  transfers between devices with their start and end apart: 7 -> 9, of which waited for: 7 -> 9; matrix products, arithmetic and copies ran while one was open for 1% -> 1% of each run, Pallas kernels for 0% -> 0%
where the time goes in v1:
time: 787 us; the launch traced here: 784 us
  waiting for transfers between devices  611 us (78%)
  local copies, waits for them, and re-layouts  121 us (15%)
  other arithmetic  28.1 us (4%)
  between operations  14 us (2%)
    reduce_scatter x1, waiting for transfers between devices, body(): lax.psum_scatter(partial_value, 'feat', scatter_dimension=0, tiled=True)  221 us
    reduce_scatter x1, waiting for transfers between devices, body(): lax.psum_scatter(table_grad.astype(jnp.bfloat16), 'feat', scatter_dimensi...  215 us
    gather x16, local copies, waits for them, and re-layouts, mean_rows(): picked = table[nbrs[:, slot]].astype(jnp.float32)  106 us
    all_gather x1, waiting for transfers between devices, body(): grad_pre_first = lax.all_gather(grad_pre_own, 'feat', axis=0, tiled=True)  76.1 us
    all_gather x1, waiting for transfers between devices, body(): table = lax.all_gather(hidden_own, 'feat', axis=0, tiled=True)  75.6 us
    ppermute x3, waiting for transfers between devices, body(): lax.ppermute(grad_first, 'dp', [(i_2, i_2 ^ far) for i_2 in range(n_dev)])  16.5 us
  transfers between devices with their start and end apart: 9, of which 9 were waited for; matrix products, arithmetic and copies ran while one was open for 1% of the time, Pallas kernels for 0%

profile of v1, /device:TPU:8, one launch (start us, length us, event | category | flops | bytes accessed | tf_op | source)
XLA Modules:
  0.0 784.5 jit_solution(14976294516062658510)
XLA Ops:
  8.7 4.6 copy.22
  13.4 11.1 %gather_fusion = bf16[2048,320]{1,0:T(8,128)(2,1)} fusion(bf16[4096,320]{1,0:T(8,128)(2,1)} %copy.22, s32[2048]{0:T(1024)S(1)} %broadcast_clamp_fusion.7), kind=kCustom, calls=%fused_computation | custom fusion | bytes 2629632 | tf_op jit(solution)/shard_map/gather | solution.py:20
  24.5 11.1 %gather_fusion.1 = bf16[2048,320]{1,0:T(8,128)(2,1)} fusion(bf16[4096,320]{1,0:T(8,128)(2,1)} %copy.22, s32[2048]{0:T(1024)S(1)} %broadcast_clamp_fusion.6), kind=kCustom, calls=%fused_computation.1 | custom fusion | bytes 2629632 | tf_op jit(solution)/shard_map/gather | solution.py:20
  35.7 11.2 %gather_fusion.2 = bf16[2048,320]{1,0:T(8,128)(2,1)} fusion(bf16[4096,320]{1,0:T(8,128)(2,1)} %copy.22, s32[2048]{0:T(1024)S(1)} %broadcast_clamp_fusion.5), kind=kCustom, calls=%fused_computation.2 | custom fusion | bytes 2629632 | tf_op jit(solution)/shard_map/gather | solution.py:20
  46.8 11.2 %gather_fusion.3 = bf16[2048,320]{1,0:T(8,128)(2,1)} fusion(bf16[4096,320]{1,0:T(8,128)(2,1)} %copy.22, s32[2048]{0:T(1024)S(1)} %broadcast_clamp_fusion.4), kind=kCustom, calls=%fused_computation.3 | custom fusion | bytes 2629632 | tf_op jit(solution)/shard_map/gather | solution.py:20
  58.0 11.2 %gather_fusion.4 = bf16[2048,320]{1,0:T(8,128)(2,1)} fusion(bf16[4096,320]{1,0:T(8,128)(2,1)} %copy.22, s32[2048]{0:T(1024)S(1)} %broadcast_clamp_fusion.3), kind=kCustom, calls=%fused_computation.4 | custom fusion | bytes 2629632 | tf_op jit(solution)/shard_map/gather | solution.py:20
  69.2 11.1 %gather_fusion.5 = bf16[2048,320]{1,0:T(8,128)(2,1)} fusion(bf16[4096,320]{1,0:T(8,128)(2,1)} %copy.22, s32[2048]{0:T(1024)S(1)} %broadcast_clamp_fusion.2), kind=kCustom, calls=%fused_computation.5 | custom fusion | bytes 2629632 | tf_op jit(solution)/shard_map/gather | solution.py:20
  80.3 11.1 %gather_fusion.6 = bf16[2048,320]{1,0:T(8,128)(2,1)} fusion(bf16[4096,320]{1,0:T(8,128)(2,1)} %copy.22, s32[2048]{0:T(1024)S(1)} %broadcast_clamp_fusion.1), kind=kCustom, calls=%fused_computation.6 | custom fusion | bytes 2629632 | tf_op jit(solution)/shard_map/gather | solution.py:20
  91.5 11.2 %gather_fusion.7 = bf16[2048,320]{1,0:T(8,128)(2,1)} fusion(bf16[4096,320]{1,0:T(8,128)(2,1)} %copy.22, s32[2048]{0:T(1024)S(1)} %broadcast_clamp_fusion), kind=kCustom, calls=%fused_computation.7 | custom fusion | bytes 2629632 | tf_op jit(solution)/shard_map/gather | solution.py:20
  102.6 8.9 %add_convert_fusion = bf16[2048,320]{1,0:T(8,128)(2,1)S(1)} fusion(bf16[2048,320]{1,0:T(8,128)(2,1)} %gather_fusion.7, bf16[2048,320]{1,0:T(8,128)(2,1)} %gather_fusion.6, bf16[2048,320]{1,0:T(8,128)(2,1)} %gather_fusion.5, bf16[2048,320]{1,0:T(8,128)(2,1)} %gather_fusion.4, bf16[2048,320]{1,0:T(8,128)(2,1)} %gather_fusion.3, ...), kind=kLoop, calls=%fused_computation.19 | loop fusion | flops 17694720 | bytes 13131776 | tf_op jit(solution)/shard_map/convert_element_type | solution.py:50
  111.6 2.0 fusion.40
  113.7 220.8 %reduce-scatter.3.cloned.1.call-done = f32[64,256]{1,0:T(8,128)} async-done(((f32[2048,256]{1,0:T(8,128)}), f32[64,256]{1,0:T(8,128)}) %reduce-scatter.3.cloned.1.call-update) | async-done | bytes 65552 | tf_op jit(solution)/shard_map/reduce_scatter | solution.py:52
  336.5 75.6 %all-gather.3.cloned.1.call-done = bf16[2048,256]{1,0:T(8,128)(2,1)} async-done(((bf16[64,256]{1,0:T(8,128)(2,1)}), bf16[2048,256]{1,0:T(8,128)(2,1)}) %all-gather.3.cloned.1.call-update) | async-done | bytes 1048592 | tf_op jit(solution)/shard_map/all_gather | solution.py:54
  412.1 3.6 gather_fusion.8
  417.1 5.8 collective-permute-done
  423.6 2.1 gather_fusion.10
  425.8 2.2 gather_fusion.11
  428.0 2.1 gather_fusion.12
  430.1 2.1 gather_fusion.13
  432.3 2.1 gather_fusion.14
  434.4 2.1 gather_fusion.15
  436.6 2.1 gather_fusion.9
  438.7 2.1 gather_fusion.16
  441.7 5.1 scatter_custom_fusion
  447.9 3.1 slice.112
  451.7 6.0 scatter_custom_fusion.1
  457.7 2.7 convert_element_type.125
  460.5 215.1 %reduce-scatter.5.cloned.1.call-done = bf16[64,256]{1,0:T(8,128)(2,1)} async-done(((bf16[2048,256]{1,0:T(8,128)(2,1)}), bf16[64,256]{1,0:T(8,128)(2,1)}) %reduce-scatter.5.cloned.1.call-update) | async-done | bytes 32784 | tf_op jit(solution)/shard_map/reduce_scatter | solution.py:78
  677.1 76.1 %all-gather.5.cloned.1.call-done = bf16[2048,256]{1,0:T(8,128)(2,1)} async-done(((bf16[64,256]{1,0:T(8,128)(2,1)}), bf16[2048,256]{1,0:T(8,128)(2,1)}) %all-gather.5.cloned.1.call-update) | async-done | bytes 1048592 | tf_op jit(solution)/shard_map/all_gather | solution.py:84
  758.4 8.3 %collective-permute-done.3 = f32[320,256]{1,0:T(8,128)S(1)} collective-permute-done((f32[320,256]{1,0:T(8,128)S(1)}, f32[320,256]{1,0:T(8,128)S(1)}, u32[]{:S(2)}, u32[]{:S(2)}) %collective-permute-start.3) | collective-permute-done | bytes 327712 | tf_op jit(solution)/shard_map/ppermute | solution.py:91
  766.7 3.1 collective-permute-start.4
  770.6 6.6 collective-permute-done.4
  (75 shorter events, 16.6 us)
Async XLA Ops:
  7.2 433.7 %copy-start = (bf16[256,1024]{1,0:T(8,128)(2,1)S(1)}, bf16[256,1024]{1,0:T(8,128)(2,1)}, u32[]{:S(2)}) copy-start(bf16[256,1024]{1,0:T(8,128)(2,1)} %param.19) | copy-start | bytes 1572868
  7.2 327.3 %reduce-scatter.3.cloned.1.call-start = ((), (), s32[]{:S(2)}) async-start(), calls=%async_computation.2 | async-start | bytes 2162688 | tf_op jit(solution)/shard_map/reduce_scatter | solution.py:52
  8.7 4.6 copy-start.5
  102.6 8.9 %copy-start.3 = (bf16[320,256]{1,0:T(8,128)(2,1)S(1)}, bf16[320,256]{1,0:T(8,128)(2,1)}, u32[]{:S(2)}) copy-start(bf16[320,256]{1,0:T(8,128)(2,1)} %param.14) | copy-start | bytes 491524
  113.6 220.9 %copy-start.8 = (f32[256]{0:T(256)S(1)}, f32[256]{0:T(256)}, u32[]{:S(2)}) copy-start(f32[256]{0:T(256)} %param.15) | copy-start | bytes 3076
  113.6 222.6 %copy-start.10 = (s32[512]{0:T(512)S(1)}, s32[512]{0:T(512)}, u32[]{:S(2)}) copy-start(s32[512]{0:T(512)} %param.16) | copy-start | bytes 6148
  113.6 222.7 %copy-start.7 = (s32[64,8]{0,1:T(8,128)S(1)}, s32[64,8]{0,1:T(8,128)}, u32[]{:S(2)}) copy-start(s32[64,8]{0,1:T(8,128)} %param.17) | copy-start | bytes 6148
  113.6 222.7 %copy-start.9 = (s32[64]{0:T(128)S(1)}, s32[64]{0:T(128)}, u32[]{:S(2)}) copy-start(s32[64]{0:T(128)} %param.18) | copy-start | bytes 772
  113.6 298.4 %all-gather.3.cloned.1.call-start = ((), (), s32[]{:S(2)}) async-start(), calls=%async_computation.3 | async-start | bytes 1081344 | tf_op jit(solution)/shard_map/all_gather | solution.py:54
  336.0 339.7 %reduce-scatter.5.cloned.1.call-start = ((), (), s32[]{:S(2)}) async-start(), calls=%async_computation.4 | async-start | bytes 1081344 | tf_op jit(solution)/shard_map/reduce_scatter | solution.py:78
  412.1 3.9 copy-start.1
  415.7 7.2 collective-permute-start
  417.1 23.8 %copy-start.4 = (bf16[64,256]{1,0:T(8,128)(2,1)S(1)}, bf16[64,256]{1,0:T(8,128)(2,1)}, u32[]{:S(2)}) copy-start(bf16[64,256]{1,0:T(8,128)(2,1)} %multiply_convert_fusion.3) | copy-start | bytes 98308
  425.8 15.4 %copy-start.6 = (bf16[64,256]{1,0:T(8,128)(2,1)S(1)}, bf16[64,256]{1,0:T(8,128)(2,1)}, u32[]{:S(2)}) copy-start(bf16[64,256]{1,0:T(8,128)(2,1)} %param.21) | copy-start | bytes 98308
  425.8 15.4 %copy-start.11 = (bf16[1024,256]{1,0:T(8,128)(2,1)S(1)}, bf16[1024,256]{1,0:T(8,128)(2,1)}, u32[]{:S(2)}) copy-start(bf16[1024,256]{1,0:T(8,128)(2,1)} %param.20) | copy-start | bytes 1572868
  447.8 3.9 collective-permute-start.1
  457.7 217.9 %copy-start.2 = (f32[64,256]{1,0:T(8,128)S(1)}, f32[64,256]{1,0:T(8,128)}, u32[]{:S(2)}) copy-start(f32[64,256]{1,0:T(8,128)} %reduce-scatter.3.cloned.1.call-done) | copy-start | bytes 196612
  460.5 292.7 %all-gather.5.cloned.1.call-start = ((), (), s32[]{:S(2)}) async-start(), calls=%async_computation.5 | async-start | bytes 1081344 | tf_op jit(solution)/shard_map/all_gather | solution.py:84
  755.0 1.7 collective-permute-start.2
  756.8 9.8 %collective-permute-start.3 = (f32[320,256]{1,0:T(8,128)S(1)}, f32[320,256]{1,0:T(8,128)S(1)}, u32[]{:S(2)}, u32[]{:S(2)}) collective-permute-start(f32[320,256]{1,0:T(8,128)S(1)} %add.208), channel_id=1, source_target_pairs={{0,2},{1,3},{2,0},{3,1},{4,6},{5,7},{6,4},{7,5},{8,10},{9,11},{10,... | collective-permute-start | bytes 983048 | tf_op jit(solution)/shard_map/ppermute | solution.py:91
  766.7 10.5 %collective-permute-start.4 = (f32[320,256]{1,0:T(8,128)S(1)}, f32[320,256]{1,0:T(8,128)S(1)}, u32[]{:S(2)}, u32[]{:S(2)}) collective-permute-start(f32[320,256]{1,0:T(8,128)S(1)} %add.209), channel_id=1, source_target_pairs={{0,4},{1,5},{2,6},{3,7},{4,0},{5,1},{6,2},{7,3},{8,12},{9,13},{10,... | collective-permute-start | bytes 983048 | tf_op jit(solution)/shard_map/ppermute | solution.py:91
Sparse Core Ops, SparseCore 0:
  113.8 220.6 reduce-scatter.2
  337.6 74.3 all-gather.2
  460.6 215.0 reduce-scatter.4
  678.7 74.4 all-gather.4
